TPU v7x, 32 devices: a whole 2x2x4 slice. The times are simulated.
32 devices in a mesh: cen: 8 (over y, x, core), grp: 4 (over z).
Axes of the slice: x: 2, y: 2, z: 4, core: 2. Of those that a mesh axis runs over, the one named last changes fastest.
Arguments:
- centers: bfloat16 [65536, 1024], P(('cen', 'grp')), may hold values from -2 to 2
- coefficients: float32 [65536, 256], P(('cen', 'grp')), may hold values from -0.09375 to 0.09375
- batch_index: int32 [256], P(('cen', 'grp')), may hold values from 0 to 65535, as said below
- batch_labels: float32 [256, 256], P(('cen', 'grp')), may hold values from -24 to 24
- nystrom_index: int32 [16384], P(('cen', 'grp')), may hold values from 0 to 65535, as said below
- eigenvectors: float32 [16384, 512], P(('cen', 'grp')), may hold values from -0.046875 to 0.046875
- eigen_weights: float32 [512], replicated, may hold values from 0.002 to 0.05
Outputs:
- residual: float32 [256, 256], P(('cen', 'grp'))
- correction: float32 [16384, 256], P(('cen', 'grp'))
Inputs may be any that keep to these rules, and one draw needn't show every extreme that they name: `batch_index`: for each j, entries 8 * j to 8 * j + 7 are distinct rows among j * 2048 to j * 2048 + 2047. `nystrom_index`: for each j, entries 512 * j to 512 * j + 511 are distinct rows among j * 2048 to j * 2048 + 2047.
All inputs are finite; a program needn't handle non-finite values.
Results may differ from a plain program's by a relative error of at most 0.0003.
Values may be sent and summed in bfloat16 or wider, within the bound.
No kernel may reach another device: no remote copies, remote signals or barrier semaphores. Data moves between devices by JAX's collectives and lax.ppermute only.
A program may use at most 64 MiB of HBM per device.

v0:
```python
import jax
import jax.numpy as jnp
from jax import lax
from jax.sharding import PartitionSpec as P


def inner_kernel(left, right):
    scores = lax.dot_general(
        left, right, (((1,), (1,)), ((), ())), preferred_element_type=jnp.float32
    )
    return jnp.exp(scores / 32.0)


def exact_dot(left, right):
    return jnp.dot(left, right, precision=lax.Precision.HIGHEST, preferred_element_type=jnp.float32)


def body(
    centers, coefficients, batch_index, batch_labels, nystrom_index, eigenvectors, eigen_weights
):
    center_count = centers.shape[0]
    owned_rows = jnp.take(centers, batch_index % center_count, axis=0)
    batch_x = lax.all_gather(owned_rows, ("cen", "grp"), axis=0, tiled=True)
    partial_pred = exact_dot(inner_kernel(batch_x, centers), coefficients)
    nystrom_x = jnp.take(centers, nystrom_index % center_count, axis=0)
    nystrom_kernel = inner_kernel(nystrom_x, batch_x)
    batch_rows = batch_labels.shape[0]
    first_row = lax.axis_index(("cen", "grp")) * batch_rows
    own_part = lax.dynamic_slice_in_dim(partial_pred, first_row, batch_rows, 0) - batch_labels
    summand = lax.dynamic_update_slice_in_dim(partial_pred, own_part, first_row, 0)
    residual_all = lax.psum(summand, ("cen", "grp"))
    own_residual = lax.dynamic_slice_in_dim(residual_all, first_row, batch_rows, 0)
    local_products = exact_dot(nystrom_kernel, residual_all)
    projected = lax.psum(exact_dot(eigenvectors.T, local_products), ("cen", "grp"))
    correction = exact_dot(eigenvectors, eigen_weights[:, None] * projected)
    return (own_residual, correction)


def solution(mesh):
    in_specs = (
        P(("cen", "grp"), None),
        P(("cen", "grp"), None),
        P(("cen", "grp")),
        P(("cen", "grp"), None),
        P(("cen", "grp")),
        P(("cen", "grp"), None),
        P(),
    )
    out_specs = (P(("cen", "grp"), None), P(("cen", "grp"), None))
    return jax.shard_map(body, mesh=mesh, in_specs=in_specs, out_specs=out_specs, check_vma=False)
```

profile of v0, /device:TPU:0, one launch (start us, length us, event | category | flops | bytes accessed | tf_op | source)
XLA Modules:
  0.0 365.1 jit_solution(11219667917849283521)
XLA Ops:
  7.2 0.0 copy-start
  7.2 0.0 all-reduce.3.cloned.1.call-start
  7.2 0.8 compare_and_fusion.1
  8.0 3.3 gather_fusion
  11.4 0.1 broadcast_select_fusion
  11.4 73.9 %all_gather.3 = bf16[256,1024]{1,0:T(8,128)(2,1)S(1)} all-gather(bf16[8,1024]{1,0:T(8,128)(2,1)S(1)} %broadcast_select_fusion), channel_id=1, replica_groups=mesh['cen'=8,'grp'=4] {'cen','grp'}, dimensions={0}, use_global_device_ids=true | all-gather | bytes 540672 | tf_op jit(solution)/shard_map/all_gather | solution.py:23
  85.4 0.0 copy-start.3
  85.4 0.8 copy-done.3
  86.2 4.9 %fusion = f32[256,2048]{1,0:T(8,128)} fusion(bf16[256,1024]{1,0:T(8,128)(2,1)S(1)} %all_gather.3, bf16[2048,1024]{1,0:T(8,128)(2,1)} %param.7), kind=kOutput, calls=%fused_computation.3 | convolution fusion | flops 1074266112 | bytes 6815744 | tf_op jit(solution)/shard_map/dot_general | solution.py:8
  91.1 0.0 copy-done
  91.1 0.0 copy-start.4
  91.1 0.0 copy-start.6
  91.1 3.5 fusion.10
  94.6 0.0 copy-done.4
  94.6 0.0 copy-start.2
  94.6 0.7 copy-done.2
  95.3 0.0 all-reduce.3.cloned.1.call-update
  95.4 0.0 all-reduce.5.cloned.1.call-start
  95.4 0.0 copy-done.6
  95.5 6.2 %gather_fusion.1 = bf16[512,1024]{1,0:T(8,128)(2,1)} fusion(bf16[2048,1024]{1,0:T(8,128)(2,1)} %param.7, s32[1024]{0:T(1024)S(1)} %pad_clamp_fusion), kind=kCustom, calls=%fused_computation.1 | custom fusion | bytes 2099200 | tf_op jit(solution)/shard_map/jit(_take)/gather | solution.py:25
  101.7 0.0 copy-start.1
  101.7 2.8 fusion.1
  104.4 114.0 %all-reduce.3.cloned.1.call-done = f32[256,256]{1,0:T(8,128)} async-done(((f32[256,256]{1,0:T(8,128)}), f32[256,256]{1,0:T(8,128)}) %all-reduce.3.cloned.1.call-update) | async-done | bytes 262160 | tf_op jit(solution)/shard_map/psum | solution.py:31
  218.5 1.7 fusion.11
  220.2 0.0 copy-done.1
  220.2 2.6 convolution_bitcast_fusion.1
  222.8 0.0 all-reduce.5.cloned.1.call-update
  222.8 1.3 constant_dynamic-slice_fusion
  224.1 128.4 %all-reduce.5.cloned.1.call-done = f32[512,256]{1,0:T(8,128)} async-done(((f32[512,256]{1,0:T(8,128)}), f32[512,256]{1,0:T(8,128)}) %all-reduce.5.cloned.1.call-update) | async-done | bytes 524304 | tf_op jit(solution)/shard_map/psum | solution.py:34
  352.5 0.0 copy-done.5
  352.5 3.8 %convolution_bitcast_fusion = f32[512,256]{0,1:T(8,128)} fusion(f32[512,512]{1,0:T(8,128)S(1)} %copy-done.1, f32[512,256]{1,0:T(8,128)} %all-reduce.5.cloned.1.call-done, f32[512]{0:T(512)S(1)} %copy-done.5), kind=kOutput, calls=%fused_computation.6 | convolution fusion | flops 805437440 | bytes 2099200 | tf_op jit(solution)/shard_map/dot_general | solution.py:15
  356.2 2.0 copy.9
  (5 shorter events, 0.0 us)
Async XLA Ops:
  7.2 83.9 %copy-start = (f32[2048,256]{1,0:T(8,128)S(1)}, f32[2048,256]{1,0:T(8,128)}, u32[]{:S(2)}) copy-start(f32[2048,256]{1,0:T(8,128)} %param.8) | copy-start | bytes 6291460
  7.2 211.3 %all-reduce.3.cloned.1.call-start = ((), (), s32[]{:S(2)}) async-start(), calls=%async_computation | async-start | bytes 524288 | tf_op jit(solution)/shard_map/psum | solution.py:31
  85.4 0.8 copy-start.3
  91.1 3.5 copy-start.4
  91.1 4.3 %copy-start.6 = (s32[512]{0:T(512)S(1)}, s32[512]{0:T(512)}, u32[]{:S(2)}) copy-start(s32[512]{0:T(512)} %param.11) | copy-start | bytes 6148
  94.6 0.7 copy-start.2
  95.4 257.1 %all-reduce.5.cloned.1.call-start = ((), (), s32[]{:S(2)}) async-start(), calls=%async_computation.1 | async-start | bytes 1048576 | tf_op jit(solution)/shard_map/psum | solution.py:34
  101.7 118.5 %copy-start.1 = (f32[512,512]{1,0:T(8,128)S(1)}, f32[512,512]{1,0:T(8,128)}, u32[]{:S(2)}) copy-start(f32[512,512]{1,0:T(8,128)} %param.12) | copy-start | bytes 3145732
  104.4 248.0 %copy-start.5 = (f32[512]{0:T(512)S(1)}, f32[512]{0:T(512)}, u32[]{:S(2)}) copy-start(f32[512]{0:T(512)} %param.13) | copy-start | bytes 6148
Sparse Core Ops, SparseCore 0:
  95.5 122.9 all-reduce.2
  224.3 128.1 all-reduce.4
where the time goes:
time: 366 us; the launch traced here: 365 us
  waiting for transfers between devices  242 us (66%)
  blocking collectives  73.9 us (20%)
  matrix products  19.3 us (5%)
  local copies, waits for them, and re-layouts  14.4 us (4%)
  between operations  14.1 us (4%)
    psum x1, waiting for transfers between devices, body(): lax.psum(exact_dot(eigenvectors.T, local_products), ('cen', 'grp'))  128 us
    psum x1, waiting for transfers between devices, body(): residual_all = lax.psum(summand, ('cen', 'grp'))  114 us
    all_gather x1, blocking collectives, body(): batch_x = lax.all_gather(owned_rows, ('cen', 'grp'), axis=0, tiled=True)  73.9 us
    dot_general x4, matrix products, exact_dot(): jnp.dot(left, right, precision=lax.Precision.HIGHEST, preferred_element_t...  11.6 us
    dot_general x2, matrix products, inner_kernel(): lax.dot_general(left, right, (((1,), (1,)), ((), ())), preferred_element_...  7.7 us
  transfers between devices with their start and end apart: 2, of which 2 were waited for; matrix products, arithmetic and copies ran while one was open for 3% of the time, Pallas kernels for 0%

commit v1 on v0

--- a/solution.py
+++ b/solution.py
@@ -31,7 +31,8 @@
     residual_all = lax.psum(summand, ("cen", "grp"))
     own_residual = lax.dynamic_slice_in_dim(residual_all, first_row, batch_rows, 0)
     local_products = exact_dot(nystrom_kernel, residual_all)
-    projected = lax.psum(exact_dot(eigenvectors.T, local_products), ("cen", "grp"))
+    panel = exact_dot(eigenvectors.T, local_products)
+    projected = lax.psum(lax.psum(panel, "cen"), "grp")
     correction = exact_dot(eigenvectors, eigen_weights[:, None] * projected)
     return (own_residual, correction)
 

time: 366 us -> 330 us (0.902)
  waiting for transfers between devices: 242 us -> 207 us
    psum x1 -> x2, waiting for transfers between devices: 128 us -> 92.9 us  [body(): projected = lax.psum(lax.psum(panel, 'cen'), 'grp')]
  transfers between devices with their start and end apart: 2 -> 3, of which waited for: 2 -> 3; matrix products, arithmetic and copies ran while one was open for 3% -> 3% of each run, Pallas kernels for 0% -> 0%
where the time goes in v1:
time: 330 us; the launch traced here: 329 us
  waiting for transfers between devices  207 us (63%)
  blocking collectives  73.9 us (22%)
  matrix products  19.3 us (6%)
  local copies, waits for them, and re-layouts  14.4 us (4%)
  between operations  13.8 us (4%)
    psum x1, waiting for transfers between devices, body(): residual_all = lax.psum(summand, ('cen', 'grp'))  114 us
    psum x2, waiting for transfers between devices, body(): projected = lax.psum(lax.psum(panel, 'cen'), 'grp')  92.9 us
    all_gather x1, blocking collectives, body(): batch_x = lax.all_gather(owned_rows, ('cen', 'grp'), axis=0, tiled=True)  73.9 us
    dot_general x4, matrix products, exact_dot(): jnp.dot(left, right, precision=lax.Precision.HIGHEST, preferred_element_t...  11.6 us
    dot_general x2, matrix products, inner_kernel(): lax.dot_general(left, right, (((1,), (1,)), ((), ())), preferred_element_...  7.7 us
  transfers between devices with their start and end apart: 3, of which 3 were waited for; matrix products, arithmetic and copies ran while one was open for 3% of the time, Pallas kernels for 0%

profile of v1, /device:TPU:0, one launch (start us, length us, event | category | flops | bytes accessed | tf_op | source)
XLA Modules:
  0.0 329.4 jit_solution(7713597480619726172)
XLA Ops:
  7.2 0.0 copy-start
  7.2 0.0 all-reduce.4.cloned.1.call-start
  7.2 0.8 compare_and_fusion.1
  8.0 3.3 %gather_fusion = bf16[8,1024]{1,0:T(8,128)(2,1)S(1)} fusion(bf16[2048,1024]{1,0:T(8,128)(2,1)} %param.7, s32[1024]{0:T(1024)S(1)} %pad_clamp_fusion.1), kind=kCustom, calls=%fused_computation | custom fusion | bytes 32800 | tf_op jit(solution)/shard_map/jit(_take)/gather | solution.py:22
  11.4 0.1 broadcast_select_fusion
  11.4 73.9 %all_gather.3 = bf16[256,1024]{1,0:T(8,128)(2,1)S(1)} all-gather(bf16[8,1024]{1,0:T(8,128)(2,1)S(1)} %broadcast_select_fusion), channel_id=1, replica_groups=mesh['cen'=8,'grp'=4] {'cen','grp'}, dimensions={0}, use_global_device_ids=true | all-gather | bytes 540672 | tf_op jit(solution)/shard_map/all_gather | solution.py:23
  85.4 0.0 copy-start.3
  85.4 0.8 copy-done.3
  86.2 4.9 %fusion = f32[256,2048]{1,0:T(8,128)} fusion(bf16[256,1024]{1,0:T(8,128)(2,1)S(1)} %all_gather.3, bf16[2048,1024]{1,0:T(8,128)(2,1)} %param.7), kind=kOutput, calls=%fused_computation.3 | convolution fusion | flops 1074266112 | bytes 6815744 | tf_op jit(solution)/shard_map/dot_general | solution.py:8
  91.1 0.0 copy-done
  91.1 3.5 %fusion.10 = f32[256,256]{1,0:T(8,128)S(1)} fusion(f32[256,2048]{1,0:T(8,128)} %fusion, f32[2048,256]{1,0:T(8,128)S(1)} %copy-done), kind=kOutput, calls=%fused_computation.31 | convolution fusion | flops 1610612736 | bytes 4456448 | tf_op jit(solution)/shard_map/dot_general | solution.py:15
  94.6 0.0 copy-done.4
  94.6 0.0 copy-start.2
  94.6 0.7 copy-done.2
  95.3 0.0 all-reduce.4.cloned.1.call-update
  95.4 0.0 all-reduce.6.cloned.1.call-start
  95.4 0.0 copy-done.6
  95.5 6.2 %gather_fusion.1 = bf16[512,1024]{1,0:T(8,128)(2,1)} fusion(bf16[2048,1024]{1,0:T(8,128)(2,1)} %param.7, s32[1024]{0:T(1024)S(1)} %pad_clamp_fusion), kind=kCustom, calls=%fused_computation.1 | custom fusion | bytes 2099200 | tf_op jit(solution)/shard_map/jit(_take)/gather | solution.py:25
  101.7 2.8 fusion.1
  104.4 114.0 %all-reduce.4.cloned.1.call-done = f32[256,256]{1,0:T(8,128)} async-done(((f32[256,256]{1,0:T(8,128)}), f32[256,256]{1,0:T(8,128)}) %all-reduce.4.cloned.1.call-update) | async-done | bytes 262160 | tf_op jit(solution)/shard_map/psum | solution.py:31
  218.5 1.7 fusion.11
  220.2 0.0 copy-done.1
  220.2 2.6 convolution_bitcast_fusion.1
  222.8 0.0 all-reduce.6.cloned.1.call-update
  222.8 0.0 all-reduce.8.cloned.1.call-start
  222.9 54.0 %all-reduce.6.cloned.1.call-done = f32[512,256]{1,0:T(8,128)} async-done(((f32[512,256]{1,0:T(8,128)}), f32[512,256]{1,0:T(8,128)}) %all-reduce.6.cloned.1.call-update) | async-done | bytes 524304 | tf_op jit(solution)/shard_map/psum | solution.py:35
  276.8 0.0 all-reduce.8.cloned.1.call-update
  276.9 1.3 constant_dynamic-slice_fusion
  278.2 38.9 %all-reduce.8.cloned.1.call-done = f32[512,256]{1,0:T(8,128)} async-done(((f32[512,256]{1,0:T(8,128)}), f32[512,256]{1,0:T(8,128)}) %all-reduce.8.cloned.1.call-update) | async-done | bytes 524304 | tf_op jit(solution)/shard_map/psum | solution.py:35
  317.0 0.0 copy-done.5
  317.0 3.8 %convolution_bitcast_fusion = f32[512,256]{0,1:T(8,128)} fusion(f32[512,512]{1,0:T(8,128)S(1)} %copy-done.1, f32[512,256]{1,0:T(8,128)} %all-reduce.8.cloned.1.call-done, f32[512]{0:T(512)S(1)} %copy-done.5), kind=kOutput, calls=%fused_computation.6 | convolution fusion | flops 805437440 | bytes 2099200 | tf_op jit(solution)/shard_map/dot_general | solution.py:15
  320.8 2.0 copy.9
  (8 shorter events, 0.0 us)
Async XLA Ops:
  7.2 83.9 %copy-start = (f32[2048,256]{1,0:T(8,128)S(1)}, f32[2048,256]{1,0:T(8,128)}, u32[]{:S(2)}) copy-start(f32[2048,256]{1,0:T(8,128)} %param.8) | copy-start | bytes 6291460
  7.2 211.3 %all-reduce.4.cloned.1.call-start = ((), (), s32[]{:S(2)}) async-start(), calls=%async_computation | async-start | bytes 524288 | tf_op jit(solution)/shard_map/psum | solution.py:31
  85.4 0.8 copy-start.3
  91.1 3.5 %copy-start.4 = (f32[8,256]{1,0:T(8,128)S(1)}, f32[8,256]{1,0:T(8,128)}, u32[]{:S(2)}) copy-start(f32[8,256]{1,0:T(8,128)} %param.10) | copy-start | bytes 24580
  91.1 4.3 %copy-start.6 = (s32[512]{0:T(512)S(1)}, s32[512]{0:T(512)}, u32[]{:S(2)}) copy-start(s32[512]{0:T(512)} %param.11) | copy-start | bytes 6148
  94.6 0.7 copy-start.2
  95.4 181.5 %all-reduce.6.cloned.1.call-start = ((), (), s32[]{:S(2)}) async-start(), calls=%async_computation.1 | async-start | bytes 1048576 | tf_op jit(solution)/shard_map/psum | solution.py:35
  101.7 118.5 %copy-start.1 = (f32[512,512]{1,0:T(8,128)S(1)}, f32[512,512]{1,0:T(8,128)}, u32[]{:S(2)}) copy-start(f32[512,512]{1,0:T(8,128)} %param.12) | copy-start | bytes 3145732
  104.4 212.6 %copy-start.5 = (f32[512]{0:T(512)S(1)}, f32[512]{0:T(512)}, u32[]{:S(2)}) copy-start(f32[512]{0:T(512)} %param.13) | copy-start | bytes 6148
  222.8 94.2 %all-reduce.8.cloned.1.call-start = ((), (), s32[]{:S(2)}) async-start(), calls=%async_computation.2 | async-start | bytes 1048576 | tf_op jit(solution)/shard_map/psum | solution.py:35
Sparse Core Ops, SparseCore 0:
  95.5 122.9 all-reduce.3
  222.9 53.8 all-reduce.5
  279.2 37.8 all-reduce.7
